TPU v7x, 128 devices: a whole 4x4x4 slice. The times are simulated.
128 devices in a mesh: dom: 16 (over x, y), sub: 8 (over z, core).
Axes of the slice: x: 4, y: 4, z: 4, core: 2. Of those that a mesh axis runs over, the one named last changes fastest.
Arguments:
- node_state: float32 [131072, 128], P(('dom', 'sub')), may hold values from -6 to 6
- edge_state: float32 [524288, 128], P(('dom', 'sub')), may hold values from -6 to 6
- sender: int32 [524288], P(('dom', 'sub')), may hold values from 0 to 1535, as said below
- receiver: int32 [524288], P(('dom', 'sub')), may hold values from 0 to 1023, as said below
- send_rows: int32 [128, 4, 128], P(('dom', 'sub')), may hold values from 0 to 1023
- step_owner: int32 [4], replicated, may hold values from 0 to 127
- edge_weights: float32 [128, 512, 128], P(('dom', 'sub')), may hold values from -0.3125 to 0.3125
- node_weights: float32 [128, 384, 128], P(('dom', 'sub')), may hold values from -0.375 to 0.375
- step_bias: float32 [128, 6, 128], P(('dom', 'sub')), may hold values from -3 to 3
- step_gain: float32 [128, 2, 128], P(('dom', 'sub')), may hold values from 0.25 to 1.75
Outputs:
- node_out: float32 [131072, 128], P(('dom', 'sub'))
- edge_out: float32 [524288, 128], P(('dom', 'sub'))
Inputs may be any that keep to these rules, and one draw needn't show every extreme that they name: sender below 1024 names an own node of the edge's device; otherwise it names ghost row k arriving from direction j as 1024 + j * 128 + k. `receiver`: non-decreasing within each device's 4096 edges; the edges w * 512 to w * 512 + 511 of a device have receivers from w * 128 to w * 128 + 127.
All inputs are finite; a program needn't handle non-finite values.
Results may differ from a plain program's by a relative error of at most 0.00015.
Values sent between devices are 32-bit elements; how exact they have to be, the bound alone decides.
A program may use at most 64 MiB of HBM per device.

v0:
```python
import jax
import jax.numpy as jnp
from jax import lax
from jax.sharding import PartitionSpec as P

WIN = 128
STEPS = 4


def from_behind(block, axis, distance):
    devices = range(lax.axis_size(axis))
    route = [((i - distance) % len(devices), i) for i in devices]
    return lax.ppermute(block, axis, route)


def broadcast(block, axis, source):
    block = jnp.where(lax.axis_index(axis) == source, block, jnp.zeros_like(block))
    return lax.psum(block, axis)


def matmul(operand, matrix):
    return jnp.dot(
        operand, matrix, precision=lax.Precision.HIGHEST, preferred_element_type=jnp.float32
    )


def normalize(values, scale_row, shift_row):
    center = values - jnp.mean(values, axis=-1, keepdims=True)
    spread = jnp.mean(center * center, axis=-1, keepdims=True)
    return center * lax.rsqrt(spread + 1e-05) * scale_row + shift_row


def edge_update(edge_rows, source_rows, target_rows, weights, biases, gains):
    features = edge_rows.shape[1]
    hidden = matmul(edge_rows, weights[:features]) + matmul(
        source_rows, weights[features : 2 * features]
    )
    hidden = hidden + matmul(target_rows, weights[2 * features : 3 * features]) + biases[0]
    hidden = jnp.maximum(hidden, 0.0)
    result_rows = matmul(hidden, weights[3 * features :]) + biases[1]
    return edge_rows + normalize(result_rows, gains[0], biases[2])


def node_update(node_rows, incoming, weights, biases, gains):
    features = node_rows.shape[1]
    hidden = (
        matmul(node_rows, weights[:features])
        + matmul(incoming, weights[features : 2 * features])
        + biases[3]
    )
    hidden = jnp.maximum(hidden, 0.0)
    result_rows = matmul(hidden, weights[2 * features :]) + biases[4]
    return node_rows + normalize(result_rows, gains[1], biases[5])


def per_device(
    node_state,
    edge_state,
    sender,
    receiver,
    send_rows,
    step_owner,
    edge_weights,
    node_weights,
    step_bias,
    step_gain,
):
    node_rows = node_state
    edge_rows = edge_state
    rows_dev = node_rows.shape[0]
    edges_dev = edge_rows.shape[0]
    features = node_rows.shape[1]
    directions = send_rows.shape[1]
    slots = send_rows.shape[2]
    windows = rows_dev // WIN
    per_window = edges_dev // windows
    lookup_rows = rows_dev + directions * slots
    offsets = (jnp.arange(windows, dtype=jnp.int32) * WIN)[:, None]
    relative = receiver.reshape(windows, per_window) - offsets
    incidence = (relative[:, :, None] == jnp.arange(WIN, dtype=jnp.int32)[None, None, :]).astype(
        jnp.float32
    )
    pick_source = (sender[:, None] == jnp.arange(lookup_rows, dtype=jnp.int32)[None, :]).astype(
        jnp.float32
    )
    pick_outgoing = (
        send_rows[0].reshape(-1)[:, None] == jnp.arange(rows_dev, dtype=jnp.int32)[None, :]
    ).astype(jnp.float32)
    for number in range(STEPS):
        outgoing = matmul(pick_outgoing, node_rows).reshape(directions, slots, features)
        dom_lower = from_behind(outgoing[0], "dom", 1)
        dom_upper = from_behind(outgoing[1], "dom", -1)
        sub_lower = from_behind(outgoing[2], "sub", 1)
        sub_upper = from_behind(outgoing[3], "sub", -1)
        arrived = jnp.concatenate([dom_lower, dom_upper, sub_lower, sub_upper], axis=0)
        lookup = jnp.concatenate([node_rows, arrived], axis=0)
        weights_edge, weights_node, biases, gains = (
            broadcast(edge_weights[0], ("dom", "sub"), step_owner[number]),
            broadcast(node_weights[0], ("dom", "sub"), step_owner[number]),
            broadcast(step_bias[0], ("dom", "sub"), step_owner[number]),
            broadcast(step_gain[0], ("dom", "sub"), step_owner[number]),
        )
        source_rows = matmul(pick_source, lookup)
        window_nodes = node_rows.reshape(windows, WIN, features)
        target_rows = jnp.einsum(
            "bew,bwd->bed",
            incidence,
            window_nodes,
            precision=lax.Precision.HIGHEST,
            preferred_element_type=jnp.float32,
        ).reshape(edges_dev, features)
        edge_rows = edge_update(edge_rows, source_rows, target_rows, weights_edge, biases, gains)
        incoming = jnp.einsum(
            "bew,bed->bwd",
            incidence,
            edge_rows.reshape(windows, per_window, features),
            precision=lax.Precision.HIGHEST,
            preferred_element_type=jnp.float32,
        ).reshape(rows_dev, features)
        node_rows = node_update(node_rows, incoming, weights_node, biases, gains)
    return (node_rows, edge_rows)


def solution(mesh):
    in_specs = (
        P(("dom", "sub"), None),
        P(("dom", "sub"), None),
        P(("dom", "sub")),
        P(("dom", "sub")),
        P(("dom", "sub"), None, None),
        P(),
        P(("dom", "sub"), None, None),
        P(("dom", "sub"), None, None),
        P(("dom", "sub"), None, None),
        P(("dom", "sub"), None, None),
    )
    out_specs = (P(("dom", "sub"), None), P(("dom", "sub"), None))
    return jax.shard_map(
        per_device, mesh=mesh, in_specs=in_specs, out_specs=out_specs, check_vma=False
    )
```

profile of v0, /device:TPU:0, one launch (start us, length us, event | category | flops | bytes accessed | tf_op | source)
XLA Modules:
  0.0 329.2 jit_solution(11352587821235670147)
XLA Ops:
  7.2 2.2 fusion.19
  9.5 1.8 collective-permute-start
  11.2 3.7 %collective-permute-start.1 = (f32[128,128]{1,0:T(8,128)S(1)}, f32[128,128]{1,0:T(8,128)S(1)}, u32[]{:S(2)}, u32[]{:S(2)}) collective-permute-start(f32[128,128]{1,0:T(8,128)S(1)} %get-tuple-element.38), channel_id=1, source_target_pairs={{8,0},{16,8},{24,16},{32,24},{40,32},{48,40},{56,48},{64,56},{72,6... | collective-permute-start | bytes 196616 | tf_op jit(solution)/shard_map/ppermute | solution.py:13
  14.9 3.2 collective-permute-start.3
  18.1 1.4 fusion.88
  22.1 2.0 select_bitcast_fusion
  24.1 0.9 select_bitcast_fusion.4
  25.1 64.3 %all-reduce = (f32[6,128]{1,0:T(8,128)S(1)}, f32[2,128]{1,0:T(2,128)S(1)}, f32[6,128]{1,0:T(8,128)S(1)}, f32[2,128]{1,0:T(2,128)S(1)}, f32[6,128]{1,0:T(8,128)S(...) all-reduce(f32[6,128]{1,0:T(8,128)S(1)} %get-tuple-element.111, ...), channel_id=1, replica_groups=mesh['dom'=16,'sub'=8] {'dom','sub'}, use_global_device_ids=true, to_apply=%region_2.3 | all-reduce | flops 4096 | bytes 32768 | tf_op jit(solution)/shard_map/psum | solution.py:18
  89.6 1.8 fusion.27
  91.6 12.6 %fusion.3 = f32[4096,128]{1,0:T(8,128)} fusion(f32[1536,128]{1,0:T(8,128)S(1)} %constant_dynamic-update-slice_fusion, s32[4096]{0:T(1024)S(1)} %copy-done.16), kind=kOutput, calls=%fused_computation.4 | convolution fusion | flops 9669967872 | bytes 2899968 | tf_op jit(solution)/shard_map/dot_general | solution.py:22
  104.2 71.1 %all-reduce.4.cloned.1.call-done = (f32[512,128]{1,0:T(8,128)}, f32[384,128]{1,0:T(8,128)}, f32[384,128]{1,0:T(8,128)}, f32[512,128]{1,0:T(8,128)}, f32[384,128]...) async-done(((f32[512,128]{1,0:T(8,128)}, f32[384,128]{1,0:T(8,128)}, f32[384,128]{1,0:T(8,128)}, f32[512,128]{1,0:T(8,128)}, ...) | async-done | bytes 1835024 | tf_op jit(solution)/shard_map/psum | solution.py:18
  175.3 3.7 %convolution_bitcast_fusion = f32[4096,128]{0,1:T(8,128)S(1)} fusion(f32[4096,128]{1,0:T(8,128)} %param.11, f32[512,128]{1,0:T(8,128)} %get-tuple-element.10), kind=kOutput, calls=%fused_computation.29 | convolution fusion | flops 805306368 | bytes 4259840 | tf_op jit(solution)/shard_map/dot_general | solution.py:22
  179.0 2.1 convolution_add_fusion.11
  181.1 2.2 fusion.15
  183.4 3.9 %fusion.89 = (f32[4096]{0:T(1024)S(1)}, f32[4096,128]{1,0:T(8,128)S(1)}) fusion(f32[128]{0:T(128)S(1)} %get-tuple-element.70, f32[4096,128]{0,1:T(8,128)S(1)} %fusion.15, f32[512,128]{1,0:T(8,128)S(1)} %copy-done.7), kind=kOutput, calls=%fused_computation.219 | convolution fusion | flops 806350848 | bytes 4276736 | tf_op jit(solution)/shard_map/dot_general | solution.py:22
  187.3 1.7 multiply_reduce_fusion.3
  189.0 2.3 add_add_fusion.3
  191.3 1.5 fusion.26
  193.4 0.7 fusion.30
  194.1 1.1 fusion.90
  195.9 1.1 fusion.18
  197.1 1.4 collective-permute-start.4
  198.4 4.2 %collective-permute-start.5 = (f32[128,128]{1,0:T(8,128)S(1)}, f32[128,128]{1,0:T(8,128)S(1)}, u32[]{:S(2)}, u32[]{:S(2)}) collective-permute-start(f32[128,128]{1,0:T(8,128)S(1)} %get-tuple-element.34), channel_id=1, source_target_pairs={{8,0},{16,8},{24,16},{32,24},{40,32},{48,40},{56,48},{64,56},{72,6... | collective-permute-start | bytes 196616 | tf_op jit(solution)/shard_map/ppermute | solution.py:13
  202.6 3.0 collective-permute-start.7
  205.6 2.0 fusion.72
  207.6 1.8 fusion.25
  210.2 11.3 %fusion.2 = f32[4096,128]{1,0:T(8,128)S(1)} fusion(f32[1536,128]{1,0:T(8,128)S(1)} %constant_dynamic-update-slice_fusion.5, s32[4096]{0:T(1024)S(1)} %copy-done.16), kind=kOutput, calls=%fused_computation.3 | convolution fusion | flops 9669967872 | bytes 2899968 | tf_op jit(solution)/shard_map/dot_general | solution.py:22
  221.5 2.1 convolution_add_fusion.8
  223.6 2.2 fusion.13
  225.9 4.3 %fusion.91 = (f32[4096]{0:T(1024)S(1)}, f32[4096,128]{1,0:T(8,128)S(1)}) fusion(f32[128]{0:T(128)S(1)} %get-tuple-element.64, f32[4096,128]{0,1:T(8,128)S(1)} %fusion.13, f32[512,128]{1,0:T(8,128)S(1)} %copy-done.6), kind=kOutput, calls=%fused_computation.221 | convolution fusion | flops 806350848 | bytes 4276736 | tf_op jit(solution)/shard_map/dot_general | solution.py:22
  230.2 1.3 multiply_reduce_fusion.2
  231.5 2.3 add_add_fusion.2
  233.8 1.5 fusion.24
  235.3 0.6 fusion.36
  235.9 1.1 fusion.92
  237.7 1.1 fusion.17
  239.0 5.5 %collective-permute-start.9 = (f32[128,128]{1,0:T(8,128)S(1)}, f32[128,128]{1,0:T(8,128)S(1)}, u32[]{:S(2)}, u32[]{:S(2)}) collective-permute-start(f32[128,128]{1,0:T(8,128)S(1)} %get-tuple-element.30), channel_id=1, source_target_pairs={{8,0},{16,8},{24,16},{32,24},{40,32},{48,40},{56,48},{64,56},{72,6... | collective-permute-start | bytes 196616 | tf_op jit(solution)/shard_map/ppermute | solution.py:13
  244.4 3.0 collective-permute-start.11
  247.4 2.0 fusion.63
  249.4 1.8 fusion.23
  252.0 11.3 %fusion.1 = f32[4096,128]{1,0:T(8,128)S(1)} fusion(f32[1536,128]{1,0:T(8,128)S(1)} %constant_dynamic-update-slice_fusion.10, s32[4096]{0:T(1024)S(1)} %copy-done.16), kind=kOutput, calls=%fused_computation.2 | convolution fusion | flops 9669967872 | bytes 2899968 | tf_op jit(solution)/shard_map/dot_general | solution.py:22
  263.4 2.1 convolution_add_fusion.5
  265.5 2.2 fusion.11
  267.7 4.3 %fusion.93 = (f32[4096]{0:T(1024)S(1)}, f32[4096,128]{1,0:T(8,128)S(1)}) fusion(f32[128]{0:T(128)S(1)} %get-tuple-element.58, f32[4096,128]{0,1:T(8,128)S(1)} %fusion.11, f32[512,128]{1,0:T(8,128)S(1)} %copy-done.5), kind=kOutput, calls=%fused_computation.223 | convolution fusion | flops 806350848 | bytes 4276736 | tf_op jit(solution)/shard_map/dot_general | solution.py:22
  272.0 1.3 multiply_reduce_fusion.1
  273.3 2.3 add_add_fusion.1
  275.6 1.5 fusion.22
  277.1 0.6 fusion.34
  277.7 1.1 fusion.94
  279.6 1.1 fusion.16
  280.8 5.5 %collective-permute-start.13 = (f32[128,128]{1,0:T(8,128)S(1)}, f32[128,128]{1,0:T(8,128)S(1)}, u32[]{:S(2)}, u32[]{:S(2)}) collective-permute-start(f32[128,128]{1,0:T(8,128)S(1)} %get-tuple-element.26), channel_id=1, source_target_pairs={{8,0},{16,8},{24,16},{32,24},{40,32},{48,40},{56,48},{64,56},{72,6... | collective-permute-start | bytes 196616 | tf_op jit(solution)/shard_map/ppermute | solution.py:13
  286.3 3.0 collective-permute-start.15
  289.2 2.0 fusion.54
  291.3 1.8 fusion.21
  293.8 11.3 %fusion = f32[4096,128]{1,0:T(8,128)S(1)} fusion(f32[1536,128]{1,0:T(8,128)S(1)} %constant_dynamic-update-slice_fusion.15, s32[4096]{0:T(1024)S(1)} %copy-done.16), kind=kOutput, calls=%fused_computation.1 | convolution fusion | flops 9669967872 | bytes 2899968 | tf_op jit(solution)/shard_map/dot_general | solution.py:22
  305.2 2.1 convolution_add_fusion.2
  307.3 2.2 fusion.9
  309.5 4.1 %fusion.95 = (f32[4096]{0:T(1024)S(1)}, f32[4096,128]{1,0:T(8,128)S(1)}) fusion(f32[128]{0:T(128)S(1)} %get-tuple-element.52, f32[4096,128]{0,1:T(8,128)S(1)} %fusion.9, f32[512,128]{1,0:T(8,128)S(1)} %copy-done.4), kind=kOutput, calls=%fused_computation.225 | convolution fusion | flops 806350848 | bytes 4276736 | tf_op jit(solution)/shard_map/dot_general | solution.py:22
  313.7 1.3 multiply_reduce_fusion
  315.0 2.3 add_add_fusion
  317.3 1.5 fusion.20
  318.8 0.6 fusion.32
  319.5 1.1 fusion.96
  321.0 1.1 add_add_fusion.4
  (123 shorter events, 5.8 us)
Async XLA Ops:
  7.2 16.9 %copy-start.12 = (f32[1,384,128]{2,1,0:T(8,128)S(1)}, f32[1,384,128]{2,1,0:T(8,128)}, u32[]{:S(2)}) copy-start(f32[1,384,128]{2,1,0:T(8,128)} %param.17) | copy-start | bytes 589828
  7.2 168.1 %all-reduce.4.cloned.1.call-start = ((), (), s32[]{:S(2)}) async-start(), calls=%async_computation | async-start | bytes 3670016 | tf_op jit(solution)/shard_map/psum | solution.py:18
  9.5 82.0 %collective-permute-start = (f32[128,128]{1,0:T(8,128)S(1)}, f32[128,128]{1,0:T(8,128)S(1)}, u32[]{:S(2)}, u32[]{:S(2)}) collective-permute-start(f32[128,128]{1,0:T(8,128)S(1)} %get-tuple-element.39), channel_id=1, source_target_pairs={{120,0},{0,8},{8,16},{16,24},{24,32},{32,40},{40,48},{48,56},{56,6... | collective-permute-start | bytes 196616 | tf_op jit(solution)/shard_map/ppermute | solution.py:13
  11.2 80.3 %collective-permute-start.1 = (f32[128,128]{1,0:T(8,128)S(1)}, f32[128,128]{1,0:T(8,128)S(1)}, u32[]{:S(2)}, u32[]{:S(2)}) collective-permute-start(f32[128,128]{1,0:T(8,128)S(1)} %get-tuple-element.38), channel_id=1, source_target_pairs={{8,0},{16,8},{24,16},{32,24},{40,32},{48,40},{56,48},{64,56},{72,6... | collective-permute-start | bytes 196616 | tf_op jit(solution)/shard_map/ppermute | solution.py:13
  14.9 76.6 %collective-permute-start.2 = (f32[128,128]{1,0:T(8,128)S(1)}, f32[128,128]{1,0:T(8,128)S(1)}, u32[]{:S(2)}, u32[]{:S(2)}) collective-permute-start(f32[128,128]{1,0:T(8,128)S(1)} %get-tuple-element.37), channel_id=1, source_target_pairs={{7,0},{0,1},{1,2},{2,3},{3,4},{4,5},{5,6},{6,7},{15,8},{8,9},{9,10... | collective-permute-start | bytes 196616 | tf_op jit(solution)/shard_map/ppermute | solution.py:13
  14.9 76.6 %collective-permute-start.3 = (f32[128,128]{1,0:T(8,128)S(1)}, f32[128,128]{1,0:T(8,128)S(1)}, u32[]{:S(2)}, u32[]{:S(2)}) collective-permute-start(f32[128,128]{1,0:T(8,128)S(1)} %get-tuple-element.36), channel_id=1, source_target_pairs={{1,0},{2,1},{3,2},{4,3},{5,4},{6,5},{7,6},{0,7},{9,8},{10,9},{11,1... | collective-permute-start | bytes 196616 | tf_op jit(solution)/shard_map/ppermute | solution.py:13
  19.5 5.5 %copy-start.14 = (f32[1,6,128]{2,0,1:T(1,128)S(1)}, f32[1,6,128]{2,0,1:T(1,128)}, u32[]{:S(2)}) copy-start(f32[1,6,128]{2,0,1:T(1,128)} %param.18) | copy-start | bytes 9220
  20.9 4.2 %copy-start.15 = (f32[1,2,128]{2,1,0:T(2,128)S(1)}, f32[1,2,128]{2,1,0:T(2,128)}, u32[]{:S(2)}) copy-start(f32[1,2,128]{2,1,0:T(2,128)} %param.19) | copy-start | bytes 3076
  22.1 67.4 %copy-start.13 = (s32[4096]{0:T(1024)S(1)}, s32[4096]{0:T(1024)}, u32[]{:S(2)}) copy-start(s32[4096]{0:T(1024)} %param.13) | copy-start | bytes 49156
  22.1 67.5 %copy-start.2 = (f32[1024,128]{1,0:T(8,128)S(1)}, f32[1024,128]{1,0:T(8,128)}, u32[]{:S(2)}) copy-start(f32[1024,128]{1,0:T(8,128)} %param.10) | copy-start | bytes 1572868
  89.6 2.0 copy-start.16
  175.3 3.7 %copy-start.3 = (f32[4096,128]{1,0:T(8,128)S(1)}, f32[4096,128]{1,0:T(8,128)}, u32[]{:S(2)}) copy-start(f32[4096,128]{1,0:T(8,128)} %fusion.3) | copy-start | bytes 6291460
  175.3 3.7 %copy-start.7 = (f32[512,128]{1,0:T(8,128)S(1)}, f32[512,128]{1,0:T(8,128)}, u32[]{:S(2)}) copy-start(f32[512,128]{1,0:T(8,128)} %get-tuple-element.10) | copy-start | bytes 786436
  187.2 1.8 copy-start.1
  191.3 1.5 copy-start.11
  194.1 1.8 copy-start.17
  195.1 10.4 %copy-start.6 = (f32[512,128]{1,0:T(8,128)S(1)}, f32[512,128]{1,0:T(8,128)}, u32[]{:S(2)}) copy-start(f32[512,128]{1,0:T(8,128)} %get-tuple-element.13) | copy-start | bytes 786436
  197.1 13.0 %collective-permute-start.4 = (f32[128,128]{1,0:T(8,128)S(1)}, f32[128,128]{1,0:T(8,128)S(1)}, u32[]{:S(2)}, u32[]{:S(2)}) collective-permute-start(f32[128,128]{1,0:T(8,128)S(1)} %get-tuple-element.35), channel_id=1, source_target_pairs={{120,0},{0,8},{8,16},{16,24},{24,32},{32,40},{40,48},{48,56},{56,6... | collective-permute-start | bytes 196616 | tf_op jit(solution)/shard_map/ppermute | solution.py:13
  198.4 11.7 %collective-permute-start.5 = (f32[128,128]{1,0:T(8,128)S(1)}, f32[128,128]{1,0:T(8,128)S(1)}, u32[]{:S(2)}, u32[]{:S(2)}) collective-permute-start(f32[128,128]{1,0:T(8,128)S(1)} %get-tuple-element.34), channel_id=1, source_target_pairs={{8,0},{16,8},{24,16},{32,24},{40,32},{48,40},{56,48},{64,56},{72,6... | collective-permute-start | bytes 196616 | tf_op jit(solution)/shard_map/ppermute | solution.py:13
  202.6 7.5 %collective-permute-start.6 = (f32[128,128]{1,0:T(8,128)S(1)}, f32[128,128]{1,0:T(8,128)S(1)}, u32[]{:S(2)}, u32[]{:S(2)}) collective-permute-start(f32[128,128]{1,0:T(8,128)S(1)} %get-tuple-element.33), channel_id=1, source_target_pairs={{7,0},{0,1},{1,2},{2,3},{3,4},{4,5},{5,6},{6,7},{15,8},{8,9},{9,10... | collective-permute-start | bytes 196616 | tf_op jit(solution)/shard_map/ppermute | solution.py:13
  202.6 7.5 %collective-permute-start.7 = (f32[128,128]{1,0:T(8,128)S(1)}, f32[128,128]{1,0:T(8,128)S(1)}, u32[]{:S(2)}, u32[]{:S(2)}) collective-permute-start(f32[128,128]{1,0:T(8,128)S(1)} %get-tuple-element.32), channel_id=1, source_target_pairs={{1,0},{2,1},{3,2},{4,3},{5,4},{6,5},{7,6},{0,7},{9,8},{10,9},{11,1... | collective-permute-start | bytes 196616 | tf_op jit(solution)/shard_map/ppermute | solution.py:13
  207.6 1.8 copy-start.10
  237.0 10.4 %copy-start.5 = (f32[512,128]{1,0:T(8,128)S(1)}, f32[512,128]{1,0:T(8,128)}, u32[]{:S(2)}) copy-start(f32[512,128]{1,0:T(8,128)} %get-tuple-element.15) | copy-start | bytes 786436
  238.9 13.0 %collective-permute-start.8 = (f32[128,128]{1,0:T(8,128)S(1)}, f32[128,128]{1,0:T(8,128)S(1)}, u32[]{:S(2)}, u32[]{:S(2)}) collective-permute-start(f32[128,128]{1,0:T(8,128)S(1)} %get-tuple-element.31), channel_id=1, source_target_pairs={{120,0},{0,8},{8,16},{16,24},{24,32},{32,40},{40,48},{48,56},{56,6... | collective-permute-start | bytes 196616 | tf_op jit(solution)/shard_map/ppermute | solution.py:13
  239.0 13.0 %collective-permute-start.9 = (f32[128,128]{1,0:T(8,128)S(1)}, f32[128,128]{1,0:T(8,128)S(1)}, u32[]{:S(2)}, u32[]{:S(2)}) collective-permute-start(f32[128,128]{1,0:T(8,128)S(1)} %get-tuple-element.30), channel_id=1, source_target_pairs={{8,0},{16,8},{24,16},{32,24},{40,32},{48,40},{56,48},{64,56},{72,6... | collective-permute-start | bytes 196616 | tf_op jit(solution)/shard_map/ppermute | solution.py:13
  244.4 7.5 %collective-permute-start.10 = (f32[128,128]{1,0:T(8,128)S(1)}, f32[128,128]{1,0:T(8,128)S(1)}, u32[]{:S(2)}, u32[]{:S(2)}) collective-permute-start(f32[128,128]{1,0:T(8,128)S(1)} %get-tuple-element.29), channel_id=1, source_target_pairs={{7,0},{0,1},{1,2},{2,3},{3,4},{4,5},{5,6},{6,7},{15,8},{8,9},{9,10... | collective-permute-start | bytes 196616 | tf_op jit(solution)/shard_map/ppermute | solution.py:13
  244.4 7.5 %collective-permute-start.11 = (f32[128,128]{1,0:T(8,128)S(1)}, f32[128,128]{1,0:T(8,128)S(1)}, u32[]{:S(2)}, u32[]{:S(2)}) collective-permute-start(f32[128,128]{1,0:T(8,128)S(1)} %get-tuple-element.28), channel_id=1, source_target_pairs={{1,0},{2,1},{3,2},{4,3},{5,4},{6,5},{7,6},{0,7},{9,8},{10,9},{11,1... | collective-permute-start | bytes 196616 | tf_op jit(solution)/shard_map/ppermute | solution.py:13
  249.4 1.8 copy-start.9
  278.8 10.4 %copy-start.4 = (f32[512,128]{1,0:T(8,128)S(1)}, f32[512,128]{1,0:T(8,128)}, u32[]{:S(2)}) copy-start(f32[512,128]{1,0:T(8,128)} %get-tuple-element.17) | copy-start | bytes 786436
  280.7 13.0 %collective-permute-start.12 = (f32[128,128]{1,0:T(8,128)S(1)}, f32[128,128]{1,0:T(8,128)S(1)}, u32[]{:S(2)}, u32[]{:S(2)}) collective-permute-start(f32[128,128]{1,0:T(8,128)S(1)} %get-tuple-element.27), channel_id=1, source_target_pairs={{120,0},{0,8},{8,16},{16,24},{24,32},{32,40},{40,48},{48,56},{56,6... | collective-permute-start | bytes 196616 | tf_op jit(solution)/shard_map/ppermute | solution.py:13
  280.8 13.0 %collective-permute-start.13 = (f32[128,128]{1,0:T(8,128)S(1)}, f32[128,128]{1,0:T(8,128)S(1)}, u32[]{:S(2)}, u32[]{:S(2)}) collective-permute-start(f32[128,128]{1,0:T(8,128)S(1)} %get-tuple-element.26), channel_id=1, source_target_pairs={{8,0},{16,8},{24,16},{32,24},{40,32},{48,40},{56,48},{64,56},{72,6... | collective-permute-start | bytes 196616 | tf_op jit(solution)/shard_map/ppermute | solution.py:13
  286.3 7.5 %collective-permute-start.14 = (f32[128,128]{1,0:T(8,128)S(1)}, f32[128,128]{1,0:T(8,128)S(1)}, u32[]{:S(2)}, u32[]{:S(2)}) collective-permute-start(f32[128,128]{1,0:T(8,128)S(1)} %get-tuple-element.25), channel_id=1, source_target_pairs={{7,0},{0,1},{1,2},{2,3},{3,4},{4,5},{5,6},{6,7},{15,8},{8,9},{9,10... | collective-permute-start | bytes 196616 | tf_op jit(solution)/shard_map/ppermute | solution.py:13
  286.3 7.5 %collective-permute-start.15 = (f32[128,128]{1,0:T(8,128)S(1)}, f32[128,128]{1,0:T(8,128)S(1)}, u32[]{:S(2)}, u32[]{:S(2)}) collective-permute-start(f32[128,128]{1,0:T(8,128)S(1)} %get-tuple-element.24), channel_id=1, source_target_pairs={{1,0},{2,1},{3,2},{4,3},{5,4},{6,5},{7,6},{0,7},{9,8},{10,9},{11,1... | collective-permute-start | bytes 196616 | tf_op jit(solution)/shard_map/ppermute | solution.py:13
  291.3 1.8 copy-start.8
  317.3 2.2 copy-start
Sparse Core Ops, SparseCore 0:
  25.2 150.1 all-reduce.3
where the time goes:
time: 333 us; the launch traced here: 329 us
  matrix products  118 us (35%)
  waiting for transfers between devices  71.1 us (21%)
  blocking collectives  64.3 us (19%)
  starting transfers between devices  34.3 us (10%)
  other arithmetic  21.6 us (6%)
  between operations  17.9 us (5%)
    dot_general x36, matrix products, matmul(): jnp.dot(operand, matrix, precision=lax.Precision.HIGHEST, preferred_eleme...  105 us
    psum x1, waiting for transfers between devices, broadcast(): return lax.psum(block, axis)  71.1 us
    psum x1, blocking collectives, broadcast(): return lax.psum(block, axis)  64.3 us
    ppermute x16, starting transfers between devices, from_behind(): return lax.ppermute(block, axis, route)  34.2 us
    add x4, other arithmetic, edge_update(): return edge_rows + normalize(result_rows, gains[0], biases[2])  9.21 us
    dot_general x4, matrix products, per_device(): jnp.einsum('bew,bwd->bed', incidence, window_nodes, precision=lax.Precisi...  7.24 us
    reduce_sum x8, other arithmetic, normalize(): spread = jnp.mean(center * center, axis=-1, keepdims=True)  7.09 us
  transfers between devices with their start and end apart: 17, of which 1 were waited for; matrix products, arithmetic and copies ran while one was open for 10% of the time, Pallas kernels for 0%

commit v1 on v0

v1 whole, which is shorter than its diff:
```python
import jax
import jax.numpy as jnp
from jax import lax
from jax.sharding import PartitionSpec as P

WIN = 128
STEPS = 4
AXES = ("dom", "sub")


def from_behind(block, axis, distance):
    devices = range(lax.axis_size(axis))
    route = [((i - distance) % len(devices), i) for i in devices]
    return lax.ppermute(block, axis, route)


def matmul(operand, matrix):
    return jnp.dot(
        operand, matrix, precision=lax.Precision.HIGHEST, preferred_element_type=jnp.float32
    )


def normalize(values, scale_row, shift_row):
    center = values - jnp.mean(values, axis=-1, keepdims=True)
    spread = jnp.mean(center * center, axis=-1, keepdims=True)
    return center * lax.rsqrt(spread + 1e-05) * scale_row + shift_row


def per_device(
    node_state,
    edge_state,
    sender,
    receiver,
    send_rows,
    step_owner,
    edge_weights,
    node_weights,
    step_bias,
    step_gain,
):
    node_rows = node_state
    edge_rows = edge_state
    rows_dev, features = node_rows.shape
    edges_dev = edge_rows.shape[0]
    directions = send_rows.shape[1]
    slots = send_rows.shape[2]
    windows = rows_dev // WIN
    per_window = edges_dev // windows
    me = lax.axis_index("dom") * lax.axis_size("sub") + lax.axis_index("sub")

    bank = jnp.concatenate([edge_weights[0], node_weights[0], step_bias[0], step_gain[0]], axis=0)
    banks = []
    link = None
    for number in range(STEPS):
        masked = jnp.where(me == step_owner[number], bank, jnp.zeros_like(bank))
        if link is not None:
            masked, _ = lax.optimization_barrier((masked, link))
        link = lax.psum(masked, AXES)
        banks.append(link)

    offsets = (jnp.arange(windows, dtype=jnp.int32) * WIN)[:, None]
    relative = receiver.reshape(windows, per_window) - offsets
    incidence = (relative[:, :, None] == jnp.arange(WIN, dtype=jnp.int32)[None, None, :]).astype(
        jnp.float32
    )
    outgoing_rows = send_rows[0].reshape(-1)
    e_rows = 4 * features
    n_rows = 3 * features
    for number in range(STEPS):
        outgoing = jnp.take(node_rows, outgoing_rows, axis=0).reshape(directions, slots, features)
        dom_lower = from_behind(outgoing[0], "dom", 1)
        dom_upper = from_behind(outgoing[1], "dom", -1)
        sub_lower = from_behind(outgoing[2], "sub", 1)
        sub_upper = from_behind(outgoing[3], "sub", -1)
        arrived = jnp.concatenate([dom_lower, dom_upper, sub_lower, sub_upper], axis=0)

        weights = banks[number]
        w1 = weights[0:features]
        w2 = weights[features : 2 * features]
        w3 = weights[2 * features : 3 * features]
        w4 = weights[3 * features : e_rows]
        u1 = weights[e_rows : e_rows + features]
        u2 = weights[e_rows + features : e_rows + 2 * features]
        u3 = weights[e_rows + 2 * features : e_rows + n_rows]
        biases = weights[e_rows + n_rows : e_rows + n_rows + 6]
        gains = weights[e_rows + n_rows + 6 : e_rows + n_rows + 8]

        own_proj = matmul(node_rows, w2)
        ghost_proj = matmul(arrived, w2)
        source_proj = jnp.take(jnp.concatenate([own_proj, ghost_proj], axis=0), sender, axis=0)
        target_proj = jnp.take(matmul(node_rows, w3), receiver, axis=0)
        hidden = matmul(edge_rows, w1) + source_proj
        hidden = hidden + target_proj + biases[0]
        hidden = jnp.maximum(hidden, 0.0)
        result_rows = matmul(hidden, w4) + biases[1]
        edge_rows = edge_rows + normalize(result_rows, gains[0], biases[2])

        incoming = jnp.einsum(
            "bew,bed->bwd",
            incidence,
            edge_rows.reshape(windows, per_window, features),
            precision=lax.Precision.HIGHEST,
            preferred_element_type=jnp.float32,
        ).reshape(rows_dev, features)
        hidden = matmul(node_rows, u1) + matmul(incoming, u2) + biases[3]
        hidden = jnp.maximum(hidden, 0.0)
        result_rows = matmul(hidden, u3) + biases[4]
        node_rows = node_rows + normalize(result_rows, gains[1], biases[5])
    return (node_rows, edge_rows)


def solution(mesh):
    in_specs = (
        P(AXES, None),
        P(AXES, None),
        P(AXES),
        P(AXES),
        P(AXES, None, None),
        P(),
        P(AXES, None, None),
        P(AXES, None, None),
        P(AXES, None, None),
        P(AXES, None, None),
    )
    out_specs = (P(AXES, None), P(AXES, None))
    return jax.shard_map(
        per_device, mesh=mesh, in_specs=in_specs, out_specs=out_specs, check_vma=False
    )
```

time: 333 us -> 813 us (2.44)
  waiting for transfers between devices: 71.1 us -> 535 us
  local copies, waits for them, and re-layouts: 1.79 us -> 128 us
  blocking collectives: 64.3 us -> 0 us
  matrix products: 118 us -> 63.7 us
    psum x1 -> x4, waiting for transfers between devices: 71.1 us -> 535 us  [per_device(): link = lax.psum(masked, AXES)]
    gather x0 -> x12, local copies, waits for them, and re-layouts: none -> 118 us  [the longest x4 56.8 us: per_device(): target_proj = jnp.take(matmul(node_rows, w3), receiver, axis=0)]
    psum x1 -> x0, blocking collectives: 64.3 us -> none  [broadcast(): return lax.psum(block, axis)]
    dot_general x36 -> x32, matrix products: 105 us -> 57.6 us  [matmul(): jnp.dot(operand, matrix, precision=lax.Precision.HIGHEST, preferred_eleme...]
  transfers between devices with their start and end apart: 17 -> 20, of which waited for: 1 -> 4; matrix products, arithmetic and copies ran while one was open for 10% -> 2% of each run, Pallas kernels for 0% -> 0%
where the time goes in v1:
time: 813 us; the launch traced here: 801 us
  waiting for transfers between devices  535 us (66%)
  local copies, waits for them, and re-layouts  128 us (16%)
  matrix products  63.7 us (8%)
  starting transfers between devices  34.7 us (4%)
  other arithmetic  22 us (3%)
  between operations  17.6 us (2%)
    psum x4, waiting for transfers between devices, per_device(): link = lax.psum(masked, AXES)  535 us
    dot_general x32, matrix products, matmul(): jnp.dot(operand, matrix, precision=lax.Precision.HIGHEST, preferred_eleme...  57.6 us
    gather x4, local copies, waits for them, and re-layouts, per_device(): target_proj = jnp.take(matmul(node_rows, w3), receiver, axis=0)  56.8 us
    gather x4, local copies, waits for them, and re-layouts, per_device(): jnp.take(jnp.concatenate([own_proj, ghost_proj], axis=0), sender, axis=0)  56.7 us
    ppermute x16, starting transfers between devices, from_behind(): return lax.ppermute(block, axis, route)  34.5 us
  transfers between devices with their start and end apart: 20, of which 4 were waited for; matrix products, arithmetic and copies ran while one was open for 2% of the time, Pallas kernels for 0%

profile of v1, /device:TPU:0, one launch (start us, length us, event | category | flops | bytes accessed | tf_op | source)
XLA Modules:
  0.0 801.1 jit_solution(16188326950410225056)
XLA Ops:
  7.2 1.5 fusion.114
  10.0 1.9 broadcast_select_fusion.3
  13.5 1.0 gather_fusion
  14.7 1.8 collective-permute-start
  16.5 3.7 collective-permute-start.1
  20.2 3.2 collective-permute-start.3
  25.4 1.2 broadcast_select_fusion
  26.6 1.0 copy.12
  27.6 133.4 %all-reduce.5.cloned.1.call-done = f32[904,128]{1,0:T(8,128)} async-done(((f32[904,128]{1,0:T(8,128)}), f32[904,128]{1,0:T(8,128)}) %all-reduce.5.cloned.1.call-update) | async-done | bytes 462864 | tf_op jit(solution)/shard_map/psum | solution.py:58
  161.0 1.4 convolution_bitcast_fusion.2
  162.5 1.2 fusion.30
  163.7 14.2 %gather_fusion.1 = f32[4096,128]{1,0:T(8,128)} fusion(f32[1536,128]{1,0:T(8,128)S(1)} %pad_maximum_fusion, s32[4096]{0:T(1024)S(1)} %fusion.104), kind=kCustom, calls=%fused_computation.1.clone | custom fusion | bytes 4210688 | tf_op jit(solution)/shard_map/jit(_take)/gather | solution.py:90
  177.9 1.4 convolution_bitcast_fusion.1
  179.4 14.2 %gather_fusion.2 = f32[4096,128]{1,0:T(8,128)} fusion(f32[1024,128]{1,0:T(8,128)S(1)} %convolution_bitcast_fusion.1, s32[4096]{0:T(1024)S(1)} %fusion.105), kind=kCustom, calls=%fused_computation.2.clone | custom fusion | bytes 4210688 | tf_op jit(solution)/shard_map/jit(_take)/gather | solution.py:91
  194.5 5.9 fusion.12
  200.5 2.0 fusion.115
  202.5 1.3 multiply_reduce_fusion.3
  204.1 2.3 add_add_fusion.3
  206.3 1.5 fusion.16
  210.3 1.0 gather_fusion.3
  212.6 4.9 collective-permute-start.5
  217.7 2.8 collective-permute-start.7
  220.4 134.6 %all-reduce.7.cloned.1.call-done = f32[904,128]{1,0:T(8,128)} async-done(((f32[904,128]{1,0:T(8,128)}), f32[904,128]{1,0:T(8,128)}) %all-reduce.7.cloned.1.call-update) | async-done | bytes 462864 | tf_op jit(solution)/shard_map/psum | solution.py:58
  355.0 1.8 fusion.100
  356.9 1.2 fusion.38
  358.2 14.2 %gather_fusion.4 = f32[4096,128]{1,0:T(8,128)} fusion(f32[1536,128]{1,0:T(8,128)S(1)} %pad_maximum_fusion.1, s32[4096]{0:T(1024)S(1)} %fusion.104), kind=kCustom, calls=%fused_computation.6.clone | custom fusion | bytes 4210688 | tf_op jit(solution)/shard_map/jit(_take)/gather | solution.py:90
  372.3 1.8 fusion.81
  374.2 14.2 %gather_fusion.5 = f32[4096,128]{1,0:T(8,128)} fusion(f32[1024,128]{1,0:T(8,128)S(1)} %fusion.81, s32[4096]{0:T(1024)S(1)} %fusion.105), kind=kCustom, calls=%fused_computation.9.clone | custom fusion | bytes 4210688 | tf_op jit(solution)/shard_map/jit(_take)/gather | solution.py:91
  388.4 1.0 slice_bitcast_fusion.17
  389.4 5.9 fusion.8
  395.3 2.0 fusion.117
  397.3 1.3 multiply_reduce_fusion.2
  398.8 2.3 add_add_fusion.2
  401.1 1.5 fusion.15
  405.1 1.0 gather_fusion.6
  407.1 2.2 collective-permute-start.11
  410.2 4.6 collective-permute-start.9
  414.8 135.0 %all-reduce.9.cloned.1.call-done = f32[904,128]{1,0:T(8,128)} async-done(((f32[904,128]{1,0:T(8,128)}), f32[904,128]{1,0:T(8,128)}) %all-reduce.9.cloned.1.call-update) | async-done | bytes 462864 | tf_op jit(solution)/shard_map/psum | solution.py:58
  549.8 1.8 fusion.97
  551.7 1.2 fusion.46
  553.0 14.2 %gather_fusion.7 = f32[4096,128]{1,0:T(8,128)} fusion(f32[1536,128]{1,0:T(8,128)S(1)} %pad_maximum_fusion.2, s32[4096]{0:T(1024)S(1)} %fusion.104), kind=kCustom, calls=%fused_computation.7.clone | custom fusion | bytes 4210688 | tf_op jit(solution)/shard_map/jit(_take)/gather | solution.py:90
  567.2 1.8 fusion.73
  569.0 14.2 %gather_fusion.8 = f32[4096,128]{1,0:T(8,128)} fusion(f32[1024,128]{1,0:T(8,128)S(1)} %fusion.73, s32[4096]{0:T(1024)S(1)} %fusion.105), kind=kCustom, calls=%fused_computation.10.clone | custom fusion | bytes 4210688 | tf_op jit(solution)/shard_map/jit(_take)/gather | solution.py:91
  584.2 5.9 fusion.5
  590.1 2.0 fusion.119
  592.1 1.3 multiply_reduce_fusion.1
  593.7 2.3 add_add_fusion.1
  595.9 1.5 fusion.14
  600.2 1.3 add_add_fusion.5
  601.7 1.0 gather_fusion.9
  603.9 4.7 collective-permute-start.13
  608.7 2.8 collective-permute-start.15
  611.5 132.2 %all-reduce.11.cloned.1.call-done = f32[904,128]{1,0:T(8,128)} async-done(((f32[904,128]{1,0:T(8,128)}), f32[904,128]{1,0:T(8,128)}) %all-reduce.11.cloned.1.call-update) | async-done | bytes 462864 | tf_op jit(solution)/shard_map/psum | solution.py:58
  743.7 1.8 fusion.94
  745.6 1.2 fusion.54
  746.9 14.2 %gather_fusion.10 = f32[4096,128]{1,0:T(8,128)} fusion(f32[1536,128]{1,0:T(8,128)S(1)} %pad_maximum_fusion.3, s32[4096]{0:T(1024)S(1)} %fusion.104), kind=kCustom, calls=%fused_computation.8.clone | custom fusion | bytes 4210688 | tf_op jit(solution)/shard_map/jit(_take)/gather | solution.py:90
  761.1 1.8 fusion.65
  762.9 14.2 %gather_fusion.11 = f32[4096,128]{1,0:T(8,128)} fusion(f32[1024,128]{1,0:T(8,128)S(1)} %fusion.65, s32[4096]{0:T(1024)S(1)} %fusion.105), kind=kCustom, calls=%fused_computation.11.clone | custom fusion | bytes 4210688 | tf_op jit(solution)/shard_map/jit(_take)/gather | solution.py:91
  778.1 5.9 fusion.2
  784.0 2.0 fusion.121
  786.0 1.3 multiply_reduce_fusion
  787.3 2.3 add_add_fusion
  789.7 1.5 fusion.13
  793.4 1.0 copy.16
  (140 shorter events, 20.9 us)
Async XLA Ops:
  7.2 6.3 copy-start.4
  7.2 153.8 %all-reduce.5.cloned.1.call-start = ((), (), s32[]{:S(2)}) async-start(), calls=%async_computation | async-start | bytes 925696 | tf_op jit(solution)/shard_map/psum | solution.py:58
  11.9 11.5 %copy-start.20 = (s32[4096]{0:T(1024)S(1)}, s32[4096]{0:T(1024)}, u32[]{:S(2)}) copy-start(s32[4096]{0:T(1024)} %param.19) | copy-start | bytes 49156
  11.9 11.5 %copy-start.21 = (s32[4096]{0:T(1024)S(1)}, s32[4096]{0:T(1024)}, u32[]{:S(2)}) copy-start(s32[4096]{0:T(1024)} %param.18) | copy-start | bytes 49156
  11.9 13.5 %copy-start.14 = (f32[1,512,128]{2,1,0:T(8,128)S(1)}, f32[1,512,128]{2,1,0:T(8,128)}, u32[]{:S(2)}) copy-start(f32[1,512,128]{2,1,0:T(8,128)} %param.22) | copy-start | bytes 786436
  11.9 13.5 %copy-start.15 = (f32[1,384,128]{2,1,0:T(8,128)S(1)}, f32[1,384,128]{2,1,0:T(8,128)}, u32[]{:S(2)}) copy-start(f32[1,384,128]{2,1,0:T(8,128)} %param.23) | copy-start | bytes 589828
  11.9 13.5 %copy-start.22 = (f32[1,2,128]{2,1,0:T(2,128)S(1)}, f32[1,2,128]{2,1,0:T(2,128)}, u32[]{:S(2)}) copy-start(f32[1,2,128]{2,1,0:T(2,128)} %param.25) | copy-start | bytes 3076
  11.9 343.1 %all-reduce.7.cloned.1.call-start = ((), (), s32[]{:S(2)}) async-start(), calls=%async_computation.1 | async-start | bytes 925696 | tf_op jit(solution)/shard_map/psum | solution.py:58
  14.7 147.7 %collective-permute-start = (f32[128,128]{1,0:T(8,128)S(1)}, f32[128,128]{1,0:T(8,128)S(1)}, u32[]{:S(2)}, u32[]{:S(2)}) collective-permute-start(f32[128,128]{1,0:T(8,128)S(1)} %get-tuple-element.60), channel_id=1, source_target_pairs={{120,0},{0,8},{8,16},{16,24},{24,32},{32,40},{40,48},{48,56},{56,6... | collective-permute-start | bytes 196616 | tf_op jit(solution)/shard_map/ppermute | solution.py:14
  16.5 146.0 %collective-permute-start.1 = (f32[128,128]{1,0:T(8,128)S(1)}, f32[128,128]{1,0:T(8,128)S(1)}, u32[]{:S(2)}, u32[]{:S(2)}) collective-permute-start(f32[128,128]{1,0:T(8,128)S(1)} %get-tuple-element.63), channel_id=1, source_target_pairs={{8,0},{16,8},{24,16},{32,24},{40,32},{48,40},{56,48},{64,56},{72,6... | collective-permute-start | bytes 196616 | tf_op jit(solution)/shard_map/ppermute | solution.py:14
  20.2 142.3 %collective-permute-start.2 = (f32[128,128]{1,0:T(8,128)S(1)}, f32[128,128]{1,0:T(8,128)S(1)}, u32[]{:S(2)}, u32[]{:S(2)}) collective-permute-start(f32[128,128]{1,0:T(8,128)S(1)} %get-tuple-element.62), channel_id=1, source_target_pairs={{7,0},{0,1},{1,2},{2,3},{3,4},{4,5},{5,6},{6,7},{15,8},{8,9},{9,10... | collective-permute-start | bytes 196616 | tf_op jit(solution)/shard_map/ppermute | solution.py:14
  20.2 142.3 %collective-permute-start.3 = (f32[128,128]{1,0:T(8,128)S(1)}, f32[128,128]{1,0:T(8,128)S(1)}, u32[]{:S(2)}, u32[]{:S(2)}) collective-permute-start(f32[128,128]{1,0:T(8,128)S(1)} %get-tuple-element.61), channel_id=1, source_target_pairs={{1,0},{2,1},{3,2},{4,3},{5,4},{6,5},{7,6},{0,7},{9,8},{10,9},{11,1... | collective-permute-start | bytes 196616 | tf_op jit(solution)/shard_map/ppermute | solution.py:14
  179.3 15.2 %copy-start.9 = (f32[4096,128]{1,0:T(8,128)S(1)}, f32[4096,128]{1,0:T(8,128)}, u32[]{:S(2)}) copy-start(f32[4096,128]{1,0:T(8,128)} %param.17) | copy-start | bytes 6291460
  194.5 6.0 copy-start.16
  202.5 1.6 copy-start.10
  206.3 183.0 %copy-start.2 = (f32[4096,128]{1,0:T(8,128)}, f32[4096,128]{1,0:T(8,128)S(1)}, u32[]{:S(2)}) copy-start(f32[4096,128]{1,0:T(8,128)S(1)} %add_add_fusion.3) | copy-start | bytes 6291460
  207.9 2.1 copy-start.13
  210.1 192.5 %copy-start.5 = (f32[1024,128]{0,1:T(8,128)}, f32[1024,128]{0,1:T(8,128)S(1)}, u32[]{:S(2)}) copy-start(f32[1024,128]{0,1:T(8,128)S(1)} %add_add_fusion.7) | copy-start | bytes 1572868
  211.5 338.3 %all-reduce.9.cloned.1.call-start = ((), (), s32[]{:S(2)}) async-start(), calls=%async_computation.2 | async-start | bytes 925696 | tf_op jit(solution)/shard_map/psum | solution.py:58
  211.6 145.2 %collective-permute-start.4 = (f32[128,128]{1,0:T(8,128)S(1)}, f32[128,128]{1,0:T(8,128)S(1)}, u32[]{:S(2)}, u32[]{:S(2)}) collective-permute-start(f32[128,128]{1,0:T(8,128)S(1)} %get-tuple-element.56), channel_id=1, source_target_pairs={{120,0},{0,8},{8,16},{16,24},{24,32},{32,40},{40,48},{48,56},{56,6... | collective-permute-start | bytes 196616 | tf_op jit(solution)/shard_map/ppermute | solution.py:14
  212.6 144.3 %collective-permute-start.5 = (f32[128,128]{1,0:T(8,128)S(1)}, f32[128,128]{1,0:T(8,128)S(1)}, u32[]{:S(2)}, u32[]{:S(2)}) collective-permute-start(f32[128,128]{1,0:T(8,128)S(1)} %get-tuple-element.59), channel_id=1, source_target_pairs={{8,0},{16,8},{24,16},{32,24},{40,32},{48,40},{56,48},{64,56},{72,6... | collective-permute-start | bytes 196616 | tf_op jit(solution)/shard_map/ppermute | solution.py:14
  217.5 139.4 %collective-permute-start.6 = (f32[128,128]{1,0:T(8,128)S(1)}, f32[128,128]{1,0:T(8,128)S(1)}, u32[]{:S(2)}, u32[]{:S(2)}) collective-permute-start(f32[128,128]{1,0:T(8,128)S(1)} %get-tuple-element.58), channel_id=1, source_target_pairs={{7,0},{0,1},{1,2},{2,3},{3,4},{4,5},{5,6},{6,7},{15,8},{8,9},{9,10... | collective-permute-start | bytes 196616 | tf_op jit(solution)/shard_map/ppermute | solution.py:14
  217.7 139.2 %collective-permute-start.7 = (f32[128,128]{1,0:T(8,128)S(1)}, f32[128,128]{1,0:T(8,128)S(1)}, u32[]{:S(2)}, u32[]{:S(2)}) collective-permute-start(f32[128,128]{1,0:T(8,128)S(1)} %get-tuple-element.57), channel_id=1, source_target_pairs={{1,0},{2,1},{3,2},{4,3},{5,4},{6,5},{7,6},{0,7},{9,8},{10,9},{11,1... | collective-permute-start | bytes 196616 | tf_op jit(solution)/shard_map/ppermute | solution.py:14
  389.3 5.9 copy-start.18
  397.2 1.6 copy-start.3
  401.1 183.1 %copy-start = (f32[4096,128]{1,0:T(8,128)}, f32[4096,128]{1,0:T(8,128)S(1)}, u32[]{:S(2)}) copy-start(f32[4096,128]{1,0:T(8,128)S(1)} %add_add_fusion.2) | copy-start | bytes 6291460
  403.3 1.4 copy-start.6
  406.3 337.5 %all-reduce.11.cloned.1.call-start = ((), (), s32[]{:S(2)}) async-start(), calls=%async_computation.3 | async-start | bytes 925696 | tf_op jit(solution)/shard_map/psum | solution.py:58
  406.4 145.3 %collective-permute-start.10 = (f32[128,128]{1,0:T(8,128)S(1)}, f32[128,128]{1,0:T(8,128)S(1)}, u32[]{:S(2)}, u32[]{:S(2)}) collective-permute-start(f32[128,128]{1,0:T(8,128)S(1)} %get-tuple-element.54), channel_id=1, source_target_pairs={{7,0},{0,1},{1,2},{2,3},{3,4},{4,5},{5,6},{6,7},{15,8},{8,9},{9,10... | collective-permute-start | bytes 196616 | tf_op jit(solution)/shard_map/ppermute | solution.py:14
  407.1 144.6 %collective-permute-start.11 = (f32[128,128]{1,0:T(8,128)S(1)}, f32[128,128]{1,0:T(8,128)S(1)}, u32[]{:S(2)}, u32[]{:S(2)}) collective-permute-start(f32[128,128]{1,0:T(8,128)S(1)} %get-tuple-element.53), channel_id=1, source_target_pairs={{1,0},{2,1},{3,2},{4,3},{5,4},{6,5},{7,6},{0,7},{9,8},{10,9},{11,1... | collective-permute-start | bytes 196616 | tf_op jit(solution)/shard_map/ppermute | solution.py:14
  409.3 142.4 %collective-permute-start.8 = (f32[128,128]{1,0:T(8,128)S(1)}, f32[128,128]{1,0:T(8,128)S(1)}, u32[]{:S(2)}, u32[]{:S(2)}) collective-permute-start(f32[128,128]{1,0:T(8,128)S(1)} %get-tuple-element.52), channel_id=1, source_target_pairs={{120,0},{0,8},{8,16},{16,24},{24,32},{32,40},{40,48},{48,56},{56,6... | collective-permute-start | bytes 196616 | tf_op jit(solution)/shard_map/ppermute | solution.py:14
  410.2 141.5 %collective-permute-start.9 = (f32[128,128]{1,0:T(8,128)S(1)}, f32[128,128]{1,0:T(8,128)S(1)}, u32[]{:S(2)}, u32[]{:S(2)}) collective-permute-start(f32[128,128]{1,0:T(8,128)S(1)} %get-tuple-element.55), channel_id=1, source_target_pairs={{8,0},{16,8},{24,16},{32,24},{40,32},{48,40},{56,48},{64,56},{72,6... | collective-permute-start | bytes 196616 | tf_op jit(solution)/shard_map/ppermute | solution.py:14
  584.2 5.9 copy-start.19
  592.1 1.6 copy-start.1
  599.3 0.8 copy-start.12
  601.5 142.2 %copy-start.7 = (f32[1024,128]{0,1:T(8,128)}, f32[1024,128]{0,1:T(8,128)S(1)}, u32[]{:S(2)}) copy-start(f32[1024,128]{0,1:T(8,128)S(1)} %add_add_fusion.5) | copy-start | bytes 1572868
  602.9 142.6 %collective-permute-start.12 = (f32[128,128]{1,0:T(8,128)S(1)}, f32[128,128]{1,0:T(8,128)S(1)}, u32[]{:S(2)}, u32[]{:S(2)}) collective-permute-start(f32[128,128]{1,0:T(8,128)S(1)} %get-tuple-element.48), channel_id=1, source_target_pairs={{120,0},{0,8},{8,16},{16,24},{24,32},{32,40},{40,48},{48,56},{56,6... | collective-permute-start | bytes 196616 | tf_op jit(solution)/shard_map/ppermute | solution.py:14
  603.9 141.7 %collective-permute-start.13 = (f32[128,128]{1,0:T(8,128)S(1)}, f32[128,128]{1,0:T(8,128)S(1)}, u32[]{:S(2)}, u32[]{:S(2)}) collective-permute-start(f32[128,128]{1,0:T(8,128)S(1)} %get-tuple-element.51), channel_id=1, source_target_pairs={{8,0},{16,8},{24,16},{32,24},{40,32},{48,40},{56,48},{64,56},{72,6... | collective-permute-start | bytes 196616 | tf_op jit(solution)/shard_map/ppermute | solution.py:14
  608.5 137.1 %collective-permute-start.14 = (f32[128,128]{1,0:T(8,128)S(1)}, f32[128,128]{1,0:T(8,128)S(1)}, u32[]{:S(2)}, u32[]{:S(2)}) collective-permute-start(f32[128,128]{1,0:T(8,128)S(1)} %get-tuple-element.50), channel_id=1, source_target_pairs={{7,0},{0,1},{1,2},{2,3},{3,4},{4,5},{5,6},{6,7},{15,8},{8,9},{9,10... | collective-permute-start | bytes 196616 | tf_op jit(solution)/shard_map/ppermute | solution.py:14
  608.7 136.9 %collective-permute-start.15 = (f32[128,128]{1,0:T(8,128)S(1)}, f32[128,128]{1,0:T(8,128)S(1)}, u32[]{:S(2)}, u32[]{:S(2)}) collective-permute-start(f32[128,128]{1,0:T(8,128)S(1)} %get-tuple-element.49), channel_id=1, source_target_pairs={{1,0},{2,1},{3,2},{4,3},{5,4},{6,5},{7,6},{0,7},{9,8},{10,9},{11,1... | collective-permute-start | bytes 196616 | tf_op jit(solution)/shard_map/ppermute | solution.py:14
  746.9 14.2 %copy-start.8 = (f32[1024,128]{0,1:T(8,128)S(1)}, f32[1024,128]{0,1:T(8,128)}, u32[]{:S(2)}) copy-start(f32[1024,128]{0,1:T(8,128)} %copy-done.7) | copy-start | bytes 1572868
  778.1 5.9 copy-start.17
  789.6 2.8 copy-start.11
Sparse Core Ops, SparseCore 0:
  13.3 147.6 all-reduce.4
  211.7 143.2 all-reduce.6
  406.4 143.3 all-reduce.8
  600.4 143.3 all-reduce.10

commit v2 on v1

--- a/solution.py
+++ b/solution.py
@@ -12,6 +12,17 @@
     devices = range(lax.axis_size(axis))
     route = [((i - distance) % len(devices), i) for i in devices]
     return lax.ppermute(block, axis, route)
+
+
+def select_rows(choice, table):
+    first = lax.reduce_precision(table, exponent_bits=8, mantissa_bits=7)
+    rest = table - first
+    second = lax.reduce_precision(rest, exponent_bits=8, mantissa_bits=7)
+    third = lax.reduce_precision(rest - second, exponent_bits=8, mantissa_bits=7)
+    parts = jnp.concatenate([first, second, third], axis=-1).astype(jnp.bfloat16)
+    picked = jnp.matmul(choice, parts, preferred_element_type=jnp.float32)
+    width = table.shape[-1]
+    return (picked[..., :width] + picked[..., width : 2 * width]) + picked[..., 2 * width :]
 
 
 def matmul(operand, matrix):
@@ -49,14 +60,15 @@
     me = lax.axis_index("dom") * lax.axis_size("sub") + lax.axis_index("sub")
 
     bank = jnp.concatenate([edge_weights[0], node_weights[0], step_bias[0], step_gain[0]], axis=0)
-    banks = []
-    link = None
+    me_dom = lax.axis_index("dom")
+    n_sub = lax.axis_size("sub")
+    row = lax.all_gather(bank, "sub")
+    picked = []
     for number in range(STEPS):
-        masked = jnp.where(me == step_owner[number], bank, jnp.zeros_like(bank))
-        if link is not None:
-            masked, _ = lax.optimization_barrier((masked, link))
-        link = lax.psum(masked, AXES)
-        banks.append(link)
+        owner = step_owner[number]
+        column = jnp.take(row, owner % n_sub, axis=0)
+        picked.append(jnp.where(me_dom == owner // n_sub, column, jnp.zeros_like(column)))
+    banks = lax.psum(jnp.stack(picked), "dom")
 
     offsets = (jnp.arange(windows, dtype=jnp.int32) * WIN)[:, None]
     relative = receiver.reshape(windows, per_window) - offsets
@@ -64,6 +76,11 @@
         jnp.float32
     )
     outgoing_rows = send_rows[0].reshape(-1)
+    lookup_rows = rows_dev + directions * slots
+    pick_source = (sender[:, None] == jnp.arange(lookup_rows, dtype=jnp.int32)[None, :]).astype(
+        jnp.bfloat16
+    )
+    pick_target = incidence.astype(jnp.bfloat16)
     e_rows = 4 * features
     n_rows = 3 * features
     for number in range(STEPS):
@@ -87,8 +104,10 @@
 
         own_proj = matmul(node_rows, w2)
         ghost_proj = matmul(arrived, w2)
-        source_proj = jnp.take(jnp.concatenate([own_proj, ghost_proj], axis=0), sender, axis=0)
-        target_proj = jnp.take(matmul(node_rows, w3), receiver, axis=0)
+        source_proj = select_rows(pick_source, jnp.concatenate([own_proj, ghost_proj], axis=0))
+        target_proj = select_rows(
+            pick_target, matmul(node_rows, w3).reshape(windows, WIN, features)
+        ).reshape(edges_dev, features)
         hidden = matmul(edge_rows, w1) + source_proj
         hidden = hidden + target_proj + biases[0]
         hidden = jnp.maximum(hidden, 0.0)

time: 813 us -> 289 us (0.36)
  waiting for transfers between devices: 535 us -> 117 us
  local copies, waits for them, and re-layouts: 128 us -> 12.5 us
  matrix products: 63.7 us -> 86.6 us
  starting transfers between devices: 34.7 us -> 18.4 us
    psum x4 -> x1, waiting for transfers between devices: 535 us -> 83.3 us  [per_device(): banks = lax.psum(jnp.stack(picked), 'dom')]
    gather x8 -> x0, local copies, waits for them, and re-layouts: 114 us -> none  [the longest x4 56.8 us: per_device(): target_proj = jnp.take(matmul(node_rows, w3), receiver, axis=0)]
    dot_general x0 -> x8, matrix products: none -> 31.2 us  [select_rows(): picked = jnp.matmul(choice, parts, preferred_element_type=jnp.float32)]
    all_gather x0 -> x1, waiting for transfers between devices: none -> 21.5 us  [per_device(): row = lax.all_gather(bank, 'sub')]
    ppermute x16, starting transfers between devices: 34.5 us -> 18.4 us  [from_behind(): return lax.ppermute(block, axis, route)]
    ppermute x16, waiting for transfers between devices: 0.04 us -> 12.7 us  [from_behind(): return lax.ppermute(block, axis, route)]
    dot_general x32, matrix products: 57.6 us -> 49.3 us  [matmul(): jnp.dot(operand, matrix, precision=lax.Precision.HIGHEST, preferred_eleme...]
  transfers between devices with their start and end apart: 20 -> 18, of which waited for: 4 -> 5; matrix products, arithmetic and copies ran while one was open for 2% -> 5% of each run, Pallas kernels for 0% -> 0%
where the time goes in v2:
time: 289 us; the launch traced here: 285 us
  waiting for transfers between devices  117 us (40%)
  matrix products  86.6 us (30%)
  between operations  25.4 us (9%)
  other arithmetic  24.4 us (8%)
  starting transfers between devices  18.4 us (6%)
  local copies, waits for them, and re-layouts  12.5 us (4%)
    psum x1, waiting for transfers between devices, per_device(): banks = lax.psum(jnp.stack(picked), 'dom')  83.3 us
    dot_general x32, matrix products, matmul(): jnp.dot(operand, matrix, precision=lax.Precision.HIGHEST, preferred_eleme...  49.3 us
    dot_general x8, matrix products, select_rows(): picked = jnp.matmul(choice, parts, preferred_element_type=jnp.float32)  31.2 us
    all_gather x1, waiting for transfers between devices, per_device(): row = lax.all_gather(bank, 'sub')  21.5 us
    ppermute x16, starting transfers between devices, from_behind(): return lax.ppermute(block, axis, route)  18.4 us
    ppermute x16, waiting for transfers between devices, from_behind(): return lax.ppermute(block, axis, route)  12.7 us
    add x4, other arithmetic, per_device(): edge_rows = edge_rows + normalize(result_rows, gains[0], biases[2])  9.21 us
    reduce_sum x8, other arithmetic, normalize(): spread = jnp.mean(center * center, axis=-1, keepdims=True)  6.69 us
  transfers between devices with their start and end apart: 18, of which 5 were waited for; matrix products, arithmetic and copies ran while one was open for 5% of the time, Pallas kernels for 0%

profile of v2, /device:TPU:0, one launch (start us, length us, event | category | flops | bytes accessed | tf_op | source)
XLA Modules:
  0.0 284.8 jit_solution(5640044866371245829)
XLA Ops:
  7.9 1.9 pad_maximum_fusion.5
  9.8 1.5 fusion.164
  21.5 21.5 %all-gather.3.cloned.1.call-done = f32[7232,128]{1,0:T(8,128)} async-done(((f32[904,128]{1,0:T(8,128)}), f32[7232,128]{1,0:T(8,128)}) %all-gather.3.cloned.1.call-update) | async-done | bytes 3702800 | tf_op jit(solution)/shard_map/all_gather | solution.py:65
  43.0 1.6 constant_dynamic-slice_fusion.3
  45.6 1.5 pad_maximum_fusion
  50.2 4.9 %collective-permute-start.1 = (f32[128,128]{1,0:T(8,128)S(1)}, f32[128,128]{1,0:T(8,128)S(1)}, u32[]{:S(2)}, u32[]{:S(2)}) collective-permute-start(f32[128,128]{1,0:T(8,128)S(1)} %get-tuple-element.90), channel_id=1, source_target_pairs={{8,0},{16,8},{24,16},{32,24},{40,32},{48,40},{56,48},{64,56},{72,6... | collective-permute-start | bytes 196616 | tf_op jit(solution)/shard_map/ppermute | solution.py:14
  55.4 83.3 %all-reduce.2.cloned.1.call-done = f32[4,904,128]{1,2,0:T(8,128)} async-done(((f32[4,904,128]{1,2,0:T(8,128)}), f32[4,904,128]{1,2,0:T(8,128)}) %all-reduce.2.cloned.1.call-update) | async-done | bytes 1851408 | tf_op jit(solution)/shard_map/psum | solution.py:71
  138.7 1.4 convolution_bitcast_fusion.1
  141.8 1.3 copy-done.3
  144.3 6.7 %fusion.3 = f32[4096,384]{1,0:T(8,128)S(1)} fusion(s32[4096]{0:T(1024)S(1)} %copy-done.9, bf16[1536,128]{0,1:T(8,128)(2,1)S(1)} %get-tuple-element.62, bf16[1536,128]{0,1:T(8,128)(2,1)S(1)} %get-tuple-element.61, bf16[1536,128]{0,1:T(8,128)(2,1)S(1)} %get-tuple-element.60), kind=kOutput, calls=%fused_computation.8 | convolution fusion | flops 4841668608 | bytes 7487488 | tf_op jit(solution)/shard_map/dot_general | solution.py:23
  151.6 2.7 fusion.20
  154.3 2.0 fusion.165
  156.3 1.3 multiply_reduce_fusion.3
  157.7 2.3 add_add_fusion.3
  160.0 1.5 fusion.24
  162.7 1.1 fusion.166
  164.5 1.0 gather_fusion.1
  165.6 1.5 reduce-precision_convert_fusion.13
  167.1 1.1 fusion.27
  168.6 1.1 collective-permute-start.7
  169.7 2.7 collective-permute-start.5
  174.8 5.6 %collective-permute-done.4 = f32[128,128]{1,0:T(8,128)S(1)} collective-permute-done((f32[128,128]{1,0:T(8,128)S(1)}, f32[128,128]{1,0:T(8,128)S(1)}, u32[]{:S(2)}, u32[]{:S(2)}) %collective-permute-start.4) | collective-permute-done | bytes 65568 | tf_op jit(solution)/shard_map/ppermute | solution.py:14
  181.0 6.8 %fusion.2 = f32[4096,384]{1,0:T(8,128)S(1)} fusion(s32[4096]{0:T(1024)S(1)} %copy-done.9, bf16[1536,128]{1,0:T(8,128)(2,1)S(1)} %get-tuple-element.59, bf16[1536,128]{1,0:T(8,128)(2,1)S(1)} %get-tuple-element.58, bf16[1536,128]{1,0:T(8,128)(2,1)S(1)} %get-tuple-element.57), kind=kOutput, calls=%fused_computation.7 | convolution fusion | flops 4841668608 | bytes 7487488 | tf_op jit(solution)/shard_map/dot_general | solution.py:23
  187.8 2.3 fusion.16
  190.1 2.2 fusion.167
  192.3 1.3 multiply_reduce_fusion.2
  193.6 2.3 add_add_fusion.2
  196.0 1.5 fusion.23
  198.1 1.1 fusion.168
  199.9 1.0 gather_fusion.2
  201.0 1.6 reduce-precision_convert_fusion.11
  202.6 1.0 fusion.26
  204.1 2.2 collective-permute-start.11
  206.4 2.1 collective-permute-start.8
  208.5 1.4 fusion.141
  209.9 1.4 fusion.146
  211.4 2.8 collective-permute-done.8
  214.2 1.2 fusion.122
  215.6 6.8 %fusion.1 = f32[4096,384]{1,0:T(8,128)S(1)} fusion(s32[4096]{0:T(1024)S(1)} %copy-done.9, bf16[1536,128]{1,0:T(8,128)(2,1)S(1)} %get-tuple-element.56, bf16[1536,128]{1,0:T(8,128)(2,1)S(1)} %get-tuple-element.55, bf16[1536,128]{1,0:T(8,128)(2,1)S(1)} %get-tuple-element.54), kind=kOutput, calls=%fused_computation.6 | convolution fusion | flops 4841668608 | bytes 7487488 | tf_op jit(solution)/shard_map/dot_general | solution.py:23
  222.4 3.2 %fusion.13 = f32[4096,128]{1,0:T(8,128)S(1)} fusion(f32[4096,128]{1,0:T(8,128)S(1)} %bitcast.231, f32[4096,128]{1,0:T(8,128)S(1)} %copy-done.1, f32[4096,384]{1,0:T(8,128)S(1)} %fusion.1, f32[128]{0:T(128)S(1)} %get-tuple-element.30, f32[4,904,128]{1,2,0:T(8,128)} %all-reduce.2.cloned.1.call-done), kind=kOutput, calls=%fused_computation.22 | convolution fusion | flops 808452096 | bytes 12648960 | tf_op jit(solution)/shard_map/dot_general | solution.py:29
  225.6 3.2 %fusion.169 = (f32[4096]{0:T(1024)S(1)}, f32[4096,128]{1,0:T(8,128)S(1)}) fusion(f32[128]{0:T(128)S(1)} %get-tuple-element.29, f32[4096,128]{1,0:T(8,128)S(1)} %fusion.13, f32[4,904,128]{1,2,0:T(8,128)} %all-reduce.2.cloned.1.call-done), kind=kOutput, calls=%fused_computation.358 | convolution fusion | flops 806350848 | bytes 4276736 | tf_op jit(solution)/shard_map/dot_general | solution.py:29
  228.8 1.3 multiply_reduce_fusion.1
  230.2 2.3 add_add_fusion.1
  232.5 1.5 fusion.22
  234.0 1.5 fusion.35
  235.5 1.9 fusion.170
  238.1 1.0 gather_fusion.3
  239.2 1.5 reduce-precision_convert_fusion.9
  240.7 1.1 fusion.25
  242.2 1.7 collective-permute-start.15
  243.9 1.6 collective-permute-start.13
  246.1 1.4 fusion.139
  247.5 1.4 fusion.147
  249.0 4.2 %collective-permute-done.12 = f32[128,128]{1,0:T(8,128)S(1)} collective-permute-done((f32[128,128]{1,0:T(8,128)S(1)}, f32[128,128]{1,0:T(8,128)S(1)}, u32[]{:S(2)}, u32[]{:S(2)}) %collective-permute-start.12) | collective-permute-done | bytes 65568 | tf_op jit(solution)/shard_map/ppermute | solution.py:14
  253.2 1.2 fusion.130
  254.6 6.8 %fusion = f32[4096,384]{1,0:T(8,128)S(1)} fusion(s32[4096]{0:T(1024)S(1)} %copy-done.9, bf16[1536,128]{1,0:T(8,128)(2,1)S(1)} %get-tuple-element.53, bf16[1536,128]{1,0:T(8,128)(2,1)S(1)} %get-tuple-element.52, bf16[1536,128]{1,0:T(8,128)(2,1)S(1)} %get-tuple-element.51), kind=kOutput, calls=%fused_computation.5 | convolution fusion | flops 4841668608 | bytes 7487488 | tf_op jit(solution)/shard_map/dot_general | solution.py:23
  261.4 3.2 %fusion.10 = f32[4096,128]{1,0:T(8,128)S(1)} fusion(f32[4096,128]{1,0:T(8,128)S(1)} %bitcast.230, f32[4096,128]{1,0:T(8,128)S(1)} %add_add_fusion.1, f32[4096,384]{1,0:T(8,128)S(1)} %fusion, f32[128]{0:T(128)S(1)} %get-tuple-element.22, f32[4,904,128]{1,2,0:T(8,128)} %all-reduce.2.cloned.1.call-done), kind=kOutput, calls=%fused_computation.17 | convolution fusion | flops 808452096 | bytes 12648960 | tf_op jit(solution)/shard_map/dot_general | solution.py:29
  264.6 3.0 %fusion.171 = (f32[4096]{0:T(1024)S(1)}, f32[4096,128]{1,0:T(8,128)S(1)}) fusion(f32[128]{0:T(128)S(1)} %get-tuple-element.21, f32[4096,128]{1,0:T(8,128)S(1)} %fusion.10, f32[4,904,128]{1,2,0:T(8,128)} %all-reduce.2.cloned.1.call-done), kind=kOutput, calls=%fused_computation.360 | convolution fusion | flops 806350848 | bytes 4276736 | tf_op jit(solution)/shard_map/dot_general | solution.py:29
  267.6 1.3 multiply_reduce_fusion
  269.0 2.3 add_add_fusion
  271.3 1.5 fusion.21
  272.8 1.5 fusion.33
  274.3 1.9 fusion.172
  276.6 1.1 add_add_fusion.4
  (111 shorter events, 18.3 us)
Async XLA Ops:
  7.2 35.8 %all-gather.3.cloned.1.call-start = ((), (), s32[]{:S(2)}) async-start(), calls=%async_computation.1 | async-start | bytes 4165632 | tf_op jit(solution)/shard_map/all_gather | solution.py:65
  9.8 128.9 %all-reduce.2.cloned.1.call-start = ((), (), s32[]{:S(2)}) async-start(), calls=%async_computation | async-start | bytes 4194304 | tf_op jit(solution)/shard_map/psum | solution.py:71
  47.1 0.7 copy-start.8
  47.1 1.1 copy-start.2
  47.8 7.5 %copy-start.7 = (s32[4096]{0:T(1024)S(1)}, s32[4096]{0:T(1024)}, u32[]{:S(2)}) copy-start(s32[4096]{0:T(1024)} %param.17) | copy-start | bytes 49156
  49.3 94.4 %collective-permute-start.3 = (f32[128,128]{1,0:T(8,128)S(1)}, f32[128,128]{1,0:T(8,128)S(1)}, u32[]{:S(2)}, u32[]{:S(2)}) collective-permute-start(f32[128,128]{1,0:T(8,128)S(1)} %get-tuple-element.88), channel_id=1, source_target_pairs={{1,0},{2,1},{3,2},{4,3},{5,4},{6,5},{7,6},{0,7},{9,8},{10,9},{11,1... | collective-permute-start | bytes 196616 | tf_op jit(solution)/shard_map/ppermute | solution.py:14
  50.2 93.5 %collective-permute-start.2 = (f32[128,128]{1,0:T(8,128)S(1)}, f32[128,128]{1,0:T(8,128)S(1)}, u32[]{:S(2)}, u32[]{:S(2)}) collective-permute-start(f32[128,128]{1,0:T(8,128)S(1)} %get-tuple-element.89), channel_id=1, source_target_pairs={{7,0},{0,1},{1,2},{2,3},{3,4},{4,5},{5,6},{6,7},{15,8},{8,9},{9,10... | collective-permute-start | bytes 196616 | tf_op jit(solution)/shard_map/ppermute | solution.py:14
  50.2 93.5 %collective-permute-start.1 = (f32[128,128]{1,0:T(8,128)S(1)}, f32[128,128]{1,0:T(8,128)S(1)}, u32[]{:S(2)}, u32[]{:S(2)}) collective-permute-start(f32[128,128]{1,0:T(8,128)S(1)} %get-tuple-element.90), channel_id=1, source_target_pairs={{8,0},{16,8},{24,16},{32,24},{40,32},{48,40},{56,48},{64,56},{72,6... | collective-permute-start | bytes 196616 | tf_op jit(solution)/shard_map/ppermute | solution.py:14
  55.1 88.6 %collective-permute-start = (f32[128,128]{1,0:T(8,128)S(1)}, f32[128,128]{1,0:T(8,128)S(1)}, u32[]{:S(2)}, u32[]{:S(2)}) collective-permute-start(f32[128,128]{1,0:T(8,128)S(1)} %get-tuple-element.87), channel_id=1, source_target_pairs={{120,0},{0,8},{8,16},{16,24},{24,32},{32,40},{40,48},{48,56},{56,6... | collective-permute-start | bytes 196616 | tf_op jit(solution)/shard_map/ppermute | solution.py:14
  141.5 1.6 copy-start.3
  143.1 1.2 copy-start.9
  144.3 7.3 %copy-start.6 = (f32[4096,128]{1,0:T(8,128)S(1)}, f32[4096,128]{1,0:T(8,128)}, u32[]{:S(2)}) copy-start(f32[4096,128]{1,0:T(8,128)} %param.15) | copy-start | bytes 6291460
  168.2 4.6 %copy-start.4 = (f32[4,904,128]{1,2,0:T(8,128)S(1)}, f32[4,904,128]{1,2,0:T(8,128)}, u32[]{:S(2)}) copy-start(f32[4,904,128]{1,2,0:T(8,128)} %all-reduce.2.cloned.1.call-done) | copy-start | bytes 5554180
  168.6 6.1 %collective-permute-start.7 = (f32[128,128]{1,0:T(8,128)S(1)}, f32[128,128]{1,0:T(8,128)S(1)}, u32[]{:S(2)}, u32[]{:S(2)}) collective-permute-start(f32[128,128]{1,0:T(8,128)S(1)} %get-tuple-element.84), channel_id=1, source_target_pairs={{1,0},{2,1},{3,2},{4,3},{5,4},{6,5},{7,6},{0,7},{9,8},{10,9},{11,1... | collective-permute-start | bytes 196616 | tf_op jit(solution)/shard_map/ppermute | solution.py:14
  169.7 5.1 %collective-permute-start.6 = (f32[128,128]{1,0:T(8,128)S(1)}, f32[128,128]{1,0:T(8,128)S(1)}, u32[]{:S(2)}, u32[]{:S(2)}) collective-permute-start(f32[128,128]{1,0:T(8,128)S(1)} %get-tuple-element.85), channel_id=1, source_target_pairs={{7,0},{0,1},{1,2},{2,3},{3,4},{4,5},{5,6},{6,7},{15,8},{8,9},{9,10... | collective-permute-start | bytes 196616 | tf_op jit(solution)/shard_map/ppermute | solution.py:14
  169.7 5.1 %collective-permute-start.5 = (f32[128,128]{1,0:T(8,128)S(1)}, f32[128,128]{1,0:T(8,128)S(1)}, u32[]{:S(2)}, u32[]{:S(2)}) collective-permute-start(f32[128,128]{1,0:T(8,128)S(1)} %get-tuple-element.86), channel_id=1, source_target_pairs={{8,0},{16,8},{24,16},{32,24},{40,32},{48,40},{56,48},{64,56},{72,6... | collective-permute-start | bytes 196616 | tf_op jit(solution)/shard_map/ppermute | solution.py:14
  172.4 8.0 %collective-permute-start.4 = (f32[128,128]{1,0:T(8,128)S(1)}, f32[128,128]{1,0:T(8,128)S(1)}, u32[]{:S(2)}, u32[]{:S(2)}) collective-permute-start(f32[128,128]{1,0:T(8,128)S(1)} %get-tuple-element.83), channel_id=1, source_target_pairs={{120,0},{0,8},{8,16},{16,24},{24,32},{32,40},{40,48},{48,56},{56,6... | collective-permute-start | bytes 196616 | tf_op jit(solution)/shard_map/ppermute | solution.py:14
  195.9 2.2 copy-start
  204.1 7.3 %collective-permute-start.11 = (f32[128,128]{1,0:T(8,128)S(1)}, f32[128,128]{1,0:T(8,128)S(1)}, u32[]{:S(2)}, u32[]{:S(2)}) collective-permute-start(f32[128,128]{1,0:T(8,128)S(1)} %get-tuple-element.80), channel_id=1, source_target_pairs={{1,0},{2,1},{3,2},{4,3},{5,4},{6,5},{7,6},{0,7},{9,8},{10,9},{11,1... | collective-permute-start | bytes 196616 | tf_op jit(solution)/shard_map/ppermute | solution.py:14
  206.3 5.1 %collective-permute-start.10 = (f32[128,128]{1,0:T(8,128)S(1)}, f32[128,128]{1,0:T(8,128)S(1)}, u32[]{:S(2)}, u32[]{:S(2)}) collective-permute-start(f32[128,128]{1,0:T(8,128)S(1)} %get-tuple-element.81), channel_id=1, source_target_pairs={{7,0},{0,1},{1,2},{2,3},{3,4},{4,5},{5,6},{6,7},{15,8},{8,9},{9,10... | collective-permute-start | bytes 196616 | tf_op jit(solution)/shard_map/ppermute | solution.py:14
  206.3 5.1 %collective-permute-start.9 = (f32[128,128]{1,0:T(8,128)S(1)}, f32[128,128]{1,0:T(8,128)S(1)}, u32[]{:S(2)}, u32[]{:S(2)}) collective-permute-start(f32[128,128]{1,0:T(8,128)S(1)} %get-tuple-element.82), channel_id=1, source_target_pairs={{8,0},{16,8},{24,16},{32,24},{40,32},{48,40},{56,48},{64,56},{72,6... | collective-permute-start | bytes 196616 | tf_op jit(solution)/shard_map/ppermute | solution.py:14
  206.4 7.8 %collective-permute-start.8 = (f32[128,128]{1,0:T(8,128)S(1)}, f32[128,128]{1,0:T(8,128)S(1)}, u32[]{:S(2)}, u32[]{:S(2)}) collective-permute-start(f32[128,128]{1,0:T(8,128)S(1)} %get-tuple-element.79), channel_id=1, source_target_pairs={{120,0},{0,8},{8,16},{16,24},{24,32},{32,40},{40,48},{48,56},{56,6... | collective-permute-start | bytes 196616 | tf_op jit(solution)/shard_map/ppermute | solution.py:14
  215.6 6.8 %copy-start.1 = (f32[4096,128]{1,0:T(8,128)S(1)}, f32[4096,128]{1,0:T(8,128)}, u32[]{:S(2)}) copy-start(f32[4096,128]{1,0:T(8,128)} %copy-done) | copy-start | bytes 6291460
  242.2 6.7 %collective-permute-start.15 = (f32[128,128]{1,0:T(8,128)S(1)}, f32[128,128]{1,0:T(8,128)S(1)}, u32[]{:S(2)}, u32[]{:S(2)}) collective-permute-start(f32[128,128]{1,0:T(8,128)S(1)} %get-tuple-element.76), channel_id=1, source_target_pairs={{1,0},{2,1},{3,2},{4,3},{5,4},{6,5},{7,6},{0,7},{9,8},{10,9},{11,1... | collective-permute-start | bytes 196616 | tf_op jit(solution)/shard_map/ppermute | solution.py:14
  243.9 5.1 %collective-permute-start.14 = (f32[128,128]{1,0:T(8,128)S(1)}, f32[128,128]{1,0:T(8,128)S(1)}, u32[]{:S(2)}, u32[]{:S(2)}) collective-permute-start(f32[128,128]{1,0:T(8,128)S(1)} %get-tuple-element.77), channel_id=1, source_target_pairs={{7,0},{0,1},{1,2},{2,3},{3,4},{4,5},{5,6},{6,7},{15,8},{8,9},{9,10... | collective-permute-start | bytes 196616 | tf_op jit(solution)/shard_map/ppermute | solution.py:14
  243.9 5.1 %collective-permute-start.13 = (f32[128,128]{1,0:T(8,128)S(1)}, f32[128,128]{1,0:T(8,128)S(1)}, u32[]{:S(2)}, u32[]{:S(2)}) collective-permute-start(f32[128,128]{1,0:T(8,128)S(1)} %get-tuple-element.78), channel_id=1, source_target_pairs={{8,0},{16,8},{24,16},{32,24},{40,32},{48,40},{56,48},{64,56},{72,6... | collective-permute-start | bytes 196616 | tf_op jit(solution)/shard_map/ppermute | solution.py:14
  245.5 7.7 %collective-permute-start.12 = (f32[128,128]{1,0:T(8,128)S(1)}, f32[128,128]{1,0:T(8,128)S(1)}, u32[]{:S(2)}, u32[]{:S(2)}) collective-permute-start(f32[128,128]{1,0:T(8,128)S(1)} %get-tuple-element.75), channel_id=1, source_target_pairs={{120,0},{0,8},{8,16},{16,24},{24,32},{32,40},{40,48},{48,56},{56,6... | collective-permute-start | bytes 196616 | tf_op jit(solution)/shard_map/ppermute | solution.py:14
  271.3 3.0 %copy-start.5 = (f32[4096,128]{1,0:T(8,128)}, f32[4096,128]{1,0:T(8,128)S(1)}, u32[]{:S(2)}) copy-start(f32[4096,128]{1,0:T(8,128)S(1)} %add_add_fusion) | copy-start | bytes 6291460
Sparse Core Ops, SparseCore 0:
  10.2 32.7 all-gather.2
  47.2 91.4 all-reduce.1
